TPU v7x, 256 devices: a whole 4x4x8 slice. The times are simulated.
256 devices in a mesh: dp: 2 (over y_hi), expert: 128 (over x, y_lo, z, core).
Axes of the slice: x: 4, y: 4 (y_hi: 2, y_lo: 2; y = y_hi * 2 + y_lo), z: 8, core: 2. Of those that a mesh axis runs over, the one named last changes fastest.
Arguments:
- tokens: bfloat16 [4096, 4096], P(('dp', 'expert')), may hold values from -6 to 6
- routing: int32 [4096, 2], P(('dp', 'expert')), may hold values from 0 to 7, as said below
- hidden_grad: bfloat16 [131072, 512], P(('dp', 'expert')), may hold values from -3 to 3
- gate_weight: bfloat16 [4096, 65536], P(None, 'expert'), may hold values from -0.09375 to 0.09375
- up_weight: bfloat16 [4096, 65536], P(None, 'expert'), may hold values from -0.09375 to 0.09375
Outputs:
- token_grad: bfloat16 [4096, 4096], P(('dp', 'expert'))
- gate_weight_grad: bfloat16 [4096, 65536], P('dp', 'expert')
- up_weight_grad: bfloat16 [4096, 65536], P('dp', 'expert')
Inputs may be any that keep to these rules, and one draw needn't show every extreme that they name: `routing`: the 2 entries of a token differ, and no device names one expert in more than 4 of its tokens.
All inputs are finite; a program needn't handle non-finite values.
Results may differ from a plain program's by a relative error of at most 0.0085.
Values may be sent and summed in bfloat16 or wider, within the bound.
No kernel may reach another device: no remote copies, remote signals or barrier semaphores. Data moves between devices by JAX's collectives and lax.ppermute only.
A program may use at most 128 MiB of HBM per device.

v0:
```python
import jax
import jax.numpy as jnp
from jax import lax
from jax.sharding import Mesh, PartitionSpec as P

EXPERTS = 8
TOP = 2
CAP = 4


def slot_tables(routing_dev):
    flat_experts = routing_dev.reshape(-1)
    onehot = (flat_experts[:, None] == jnp.arange(EXPERTS, dtype=jnp.int32)[None, :]).astype(
        jnp.int32
    )
    before = jnp.cumsum(onehot, axis=0) - onehot
    slot_index = jnp.sum(before * onehot, axis=1)
    target = flat_experts * CAP + slot_index
    placed = target[:, None] == jnp.arange(EXPERTS * CAP, dtype=jnp.int32)[None, :]
    return placed.astype(jnp.float32)


def contract_rows(left_rows, right_rows):
    return lax.dot_general(
        left_rows, right_rows, (((0,), (0,)), ((), ())), preferred_element_type=jnp.float32
    )


def swap_dp(block):
    return lax.ppermute(block, "dp", [(0, 1), (1, 0)])


def per_device(tokens, routing, hidden_grad, gate_weight, up_weight):
    token_count, model_width = tokens.shape
    ffd = gate_weight.shape[1]
    shards = lax.axis_size("s")
    half = model_width // 2
    replica = lax.axis_index("dp")
    placed = slot_tables(routing)
    chosen = jnp.sum(placed.reshape(token_count, TOP, EXPERTS * CAP), axis=1)
    outgoing = lax.dot_general(
        chosen.astype(jnp.bfloat16),
        tokens,
        (((0,), (0,)), ((), ())),
        preferred_element_type=jnp.float32,
    ).astype(jnp.bfloat16)
    mine = lax.all_to_all(
        outgoing.reshape(EXPERTS, CAP, model_width), "e", split_axis=0, concat_axis=0, tiled=True
    ).reshape(EXPERTS * CAP, model_width)
    far_mine = swap_dp(lax.dynamic_slice_in_dim(mine, (1 - replica) * half, half, 1))
    rows = lax.all_gather(mine, "s", axis=0, tiled=True)
    far_rows = lax.all_gather(far_mine, "s", axis=0, tiled=True)
    grad_h = (
        hidden_grad.reshape(EXPERTS, shards, CAP, ffd)
        .transpose(1, 0, 2, 3)
        .reshape(-1, ffd)
        .astype(jnp.float32)
    )
    gate_pre = jnp.dot(rows, gate_weight, preferred_element_type=jnp.float32)
    up_pre = jnp.dot(rows, up_weight, preferred_element_type=jnp.float32)
    sig = jax.nn.sigmoid(gate_pre)
    gate_grad = (grad_h * up_pre * sig * (1.0 + gate_pre * (1.0 - sig))).astype(jnp.bfloat16)
    up_grad = (grad_h * gate_pre * sig).astype(jnp.bfloat16)
    grads = jnp.concatenate([gate_grad, up_grad], axis=1)
    far_grads = swap_dp(grads)
    transposed = (((1,), (1,)), ((), ()))
    partial_value = lax.dot_general(
        gate_grad, gate_weight, transposed, preferred_element_type=jnp.float32
    )
    partial_value = partial_value + lax.dot_general(
        up_grad, up_weight, transposed, preferred_element_type=jnp.float32
    )
    partial_value = partial_value.astype(jnp.bfloat16)
    summed = lax.psum_scatter(partial_value, "s", scatter_dimension=0, tiled=True)
    back = lax.all_to_all(
        summed.reshape(EXPERTS, CAP, model_width), "e", split_axis=0, concat_axis=0, tiled=True
    ).reshape(EXPERTS * CAP, model_width)
    token_grad = jnp.dot(
        chosen.astype(jnp.bfloat16), back, preferred_element_type=jnp.float32
    ).astype(jnp.bfloat16)
    own_columns = lax.dynamic_slice_in_dim(rows, replica * half, half, 1)
    own_term = lax.optimization_barrier(contract_rows(own_columns, grads).astype(jnp.bfloat16))
    weight_sum = own_term.astype(jnp.float32) + contract_rows(far_rows, far_grads)
    return (
        token_grad,
        weight_sum[:, :ffd].astype(jnp.bfloat16),
        weight_sum[:, ffd:].astype(jnp.bfloat16),
    )


def solution(mesh):
    n_dp, n_expert = mesh.devices.shape
    fine = Mesh(mesh.devices.reshape(n_dp, EXPERTS, n_expert // EXPERTS), ("dp", "e", "s"))
    all_axes = ("dp", "e", "s")
    in_specs = (
        P(all_axes, None),
        P(all_axes, None),
        P(all_axes, None),
        P(None, ("e", "s")),
        P(None, ("e", "s")),
    )
    out_specs = (P(all_axes, None), P("dp", ("e", "s")), P("dp", ("e", "s")))
    return jax.shard_map(
        per_device, mesh=fine, in_specs=in_specs, out_specs=out_specs, check_vma=False
    )
```

profile of v0, /device:TPU:16, one launch (start us, length us, event | category | flops | bytes accessed | tf_op | source)
XLA Modules:
  0.0 191.4 jit_solution(17602063873971808503)
XLA Ops:
  7.2 0.0 copy-start
  7.2 0.0 all-gather.3.cloned.1.call-start
  7.2 0.8 copy.25
  8.0 0.1 eq.29
  8.1 0.1 fusion.4
  8.2 0.1 reduce_window_sum.11
  8.2 0.2 select_reduce_fusion
  8.4 0.1 reduce_sum.21
  8.5 0.1 copy.26
  8.6 0.7 multiply_add_fusion
  9.3 0.1 convert_reduce_fusion
  9.4 0.0 copy-done
  9.4 0.2 convolution_convert_fusion
  9.6 0.1 reshape.43
  9.7 12.0 %all_to_all.10 = bf16[8,4,4096]{2,1,0:T(4,128)(2,1)S(1)} all-to-all(bf16[8,4,4096]{2,1,0:T(4,128)(2,1)S(1)} %reshape.43), channel_id=1, replica_groups=mesh['dp'=2,'e'=8,'s'=16] {'e'}, dimensions={0} | all-to-all | bytes 524288 | tf_op jit(solution)/shard_map/all_to_all | solution.py:47
  21.8 0.8 reshape.44
  22.5 0.0 all-gather.3.cloned.1.call-update
  22.6 0.0 all-gather.5.cloned.1.call-start
  22.6 0.9 constant_dynamic-slice_fusion
  23.5 0.7 collective-permute-start
  24.2 5.8 %collective-permute-done = bf16[32,2048]{1,0:T(8,128)(2,1)S(1)} collective-permute-done((bf16[32,2048]{1,0:T(8,128)(2,1)S(1)}, bf16[32,2048]{1,0:T(8,128)(2,1)S(1)}, u32[]{:S(2)}, u32[]{:S(2)}) %collective-permute-start) | collective-permute-done | bytes 131104 | tf_op jit(solution)/shard_map/ppermute | solution.py:30
  30.1 0.7 copy-done.3
  30.7 0.0 all-gather.5.cloned.1.call-update
  30.8 0.0 reduce-scatter.2.cloned.1.call-start
  30.8 1.4 reshape.48
  32.2 0.1 copy.31
  32.3 0.4 reshape.47
  32.7 0.3 copy.28
  33.0 32.5 %all-gather.3.cloned.1.call-done = bf16[512,4096]{1,0:T(8,128)(2,1)} async-done(((bf16[32,4096]{1,0:T(8,128)(2,1)}), bf16[512,4096]{1,0:T(8,128)(2,1)}) %all-gather.3.cloned.1.call-update) | async-done | bytes 4194320 | tf_op jit(solution)/shard_map/all_gather | solution.py:51
  65.5 6.1 %multiply_convert_fusion = (bf16[512,512]{0,1:T(8,128)(2,1)S(1)}, f32[512,512]{0,1:T(8,128)S(1)}) fusion(f32[512,512]{0,1:T(8,128)S(1)} %copy.28, bf16[512,4096]{1,0:T(8,128)(2,1)} %all-gather.3.cloned.1.call-done, bf16[4096,512]{1,0:T(8,128)(2,1)} %param.8), kind=kOutput, calls=%fused_computation.12 | convolution fusion | flops 2149056512 | bytes 11010048 | tf_op jit(solution)/shard_map/dot_general | solution.py:59
  71.7 0.0 copy-start.1
  71.7 2.6 %fusion.3 = bf16[512,512]{0,1:T(8,128)(2,1)S(1)} fusion(f32[512,512]{0,1:T(8,128)S(1)} %copy.28, bf16[512,4096]{1,0:T(8,128)(2,1)S(1)} %copy-done.4, bf16[4096,512]{1,0:T(8,128)(2,1)S(1)} %copy-done.2, f32[512,512]{0,1:T(8,128)S(1)} %get-tuple-element.6), kind=kOutput, calls=%fused_computation.9 | convolution fusion | flops 2150105088 | bytes 11010048 | tf_op jit(solution)/shard_map/dot_general | solution.py:60
  74.3 2.4 %fusion.9 = f32[512,4096]{1,0:T(8,128)S(1)} fusion(bf16[512,512]{0,1:T(8,128)(2,1)S(1)} %fusion.3, bf16[4096,512]{1,0:T(8,128)(2,1)S(1)} %copy-done.1), kind=kOutput, calls=%fused_computation.25 | convolution fusion | flops 2147483648 | bytes 13107200 | tf_op jit(solution)/shard_map/dot_general | solution.py:67
  76.8 4.5 %add_convert_fusion.1 = bf16[512,4096]{1,0:T(8,128)(2,1)} fusion(f32[512,4096]{1,0:T(8,128)S(1)} %fusion.9, bf16[512,512]{0,1:T(8,128)(2,1)S(1)} %get-tuple-element.5, bf16[4096,512]{1,0:T(8,128)(2,1)S(1)} %copy-done.2), kind=kOutput, calls=%fused_computation.1 | convolution fusion | flops 2151677952 | bytes 17301504 | tf_op jit(solution)/shard_map/dot_general | solution.py:70
  81.2 0.0 reduce-scatter.2.cloned.1.call-update
  81.2 0.1 pad_maximum_fusion
  81.3 0.8 collective-permute-start.1
  82.1 6.0 %convolution_convert_fusion.2 = bf16[2048,1024]{1,0:T(8,128)(2,1)} fusion(bf16[512,4096]{1,0:T(8,128)(2,1)} %all-gather.3.cloned.1.call-done, s32[]{:T(128)S(6)} %select_n.6, bf16[512,512]{0,1:T(8,128)(2,1)S(1)} %get-tuple-element.5, bf16[512,512]{0,1:T(8,128)(2,1)S(1)} %fusion.3), kind=kOutput, calls=%fused_computation.4 | convolution fusion | flops 2151677952 | bytes 7340036 | tf_op jit(solution)/shard_map/dot_general | solution.py:24
  88.1 17.9 %all-gather.5.cloned.1.call-done = bf16[512,2048]{1,0:T(8,128)(2,1)} async-done(((bf16[32,2048]{1,0:T(8,128)(2,1)}), bf16[512,2048]{1,0:T(8,128)(2,1)}) %all-gather.5.cloned.1.call-update) | async-done | bytes 2097168 | tf_op jit(solution)/shard_map/all_gather | solution.py:52
  106.0 2.4 %collective-permute-done.1 = bf16[512,1024]{0,1:T(8,128)(2,1)S(1)} collective-permute-done((bf16[512,1024]{0,1:T(8,128)(2,1)S(1)}, bf16[512,1024]{0,1:T(8,128)(2,1)S(1)}, u32[]{:S(2)}, u32[]{:S(2)}) %collective-permute-start.1) | collective-permute-done | bytes 1048608 | tf_op jit(solution)/shard_map/ppermute | solution.py:30
  108.4 7.2 %add_convert_fusion = bf16[2048,1024]{1,0:T(8,128)(2,1)} fusion(bf16[2048,1024]{1,0:T(8,128)(2,1)} %convolution_convert_fusion.2, bf16[512,2048]{1,0:T(8,128)(2,1)} %all-gather.5.cloned.1.call-done, bf16[512,1024]{0,1:T(8,128)(2,1)S(1)} %collective-permute-done.1), kind=kOutput, calls=%fused_computation | convolution fusion | flops 2153775104 | bytes 11534336 | tf_op jit(solution)/shard_map/dot_general | solution.py:24
  115.6 54.6 %reduce-scatter.2.cloned.1.call-done = bf16[32,4096]{1,0:T(8,128)(2,1)} async-done(((bf16[512,4096]{1,0:T(8,128)(2,1)}), bf16[32,4096]{1,0:T(8,128)(2,1)}) %reduce-scatter.2.cloned.1.call-update) | async-done | bytes 262160 | tf_op jit(solution)/shard_map/reduce_scatter | solution.py:74
  170.2 1.8 reshape.45
  171.9 5.1 %all-to-all-start.1 = ((bf16[8,4,4096]{2,1,0:T(4,128)(2,1)}), bf16[8,4,4096]{2,1,0:T(4,128)(2,1)S(1)}, u32[]{:S(2)}, u32[]{:S(2)}) async-start(bf16[8,4,4096]{2,1,0:T(4,128)(2,1)} %reshape.45), calls=%async_computation.2 | async-start | bytes 524288 | tf_op jit(solution)/shard_map/all_to_all | solution.py:75
  177.0 4.5 %fusion.8 = (bf16[2048,512]{1,0:T(8,128)(2,1)}, bf16[2048,512]{1,0:T(8,128)(2,1)}) fusion(bf16[2048,1024]{1,0:T(8,128)(2,1)} %add_convert_fusion), kind=kLoop, calls=%fused_computation.24 | loop fusion | bytes 8388608 | tf_op jit(solution)/shard_map/slice | solution.py:87
  181.5 2.4 %all-to-all-done.1 = bf16[8,4,4096]{2,1,0:T(4,128)(2,1)S(1)} async-done(((bf16[8,4,4096]{2,1,0:T(4,128)(2,1)}), bf16[8,4,4096]{2,1,0:T(4,128)(2,1)S(1)}, u32[]{:S(2)}, u32[]{:S(2)}) %all-to-all-start.1) | async-done | bytes 262176 | tf_op jit(solution)/shard_map/all_to_all | solution.py:75
  183.9 0.1 reshape.46
  184.0 0.8 convolution_convert_fusion.1
  (6 shorter events, 0.0 us)
Async XLA Ops:
  7.2 2.2 %copy-start = (bf16[16,4096]{1,0:T(8,128)(2,1)S(1)}, bf16[16,4096]{1,0:T(8,128)(2,1)}, u32[]{:S(2)}) copy-start(bf16[16,4096]{1,0:T(8,128)(2,1)} %param.5) | copy-start | bytes 393220
  7.2 58.4 %all-gather.3.cloned.1.call-start = ((), (), s32[]{:S(2)}) async-start(), calls=%async_computation.3 | async-start | bytes 4456448 | tf_op jit(solution)/shard_map/all_gather | solution.py:51
  22.6 83.4 %all-gather.5.cloned.1.call-start = ((), (), s32[]{:S(2)}) async-start(), calls=%async_computation.5 | async-start | bytes 2228224 | tf_op jit(solution)/shard_map/all_gather | solution.py:52
  23.5 6.6 %collective-permute-start = (bf16[32,2048]{1,0:T(8,128)(2,1)S(1)}, bf16[32,2048]{1,0:T(8,128)(2,1)S(1)}, u32[]{:S(2)}, u32[]{:S(2)}) collective-permute-start(bf16[32,2048]{1,0:T(8,128)(2,1)S(1)} %constant_dynamic-slice_fusion), channel_id=1, source_target_pairs={{0,128},{128,0},{1,129},{129,1},{2,130},{130,2},{3,131},{131,3},{4... | collective-permute-start | bytes 393224 | tf_op jit(solution)/shard_map/ppermute | solution.py:30
  30.1 0.7 copy-start.3
  30.8 139.4 %reduce-scatter.2.cloned.1.call-start = ((), (), s32[]{:S(2)}) async-start(), calls=%async_computation.4 | async-start | bytes 4456448 | tf_op jit(solution)/shard_map/reduce_scatter | solution.py:74
  65.5 6.1 %copy-start.2 = (bf16[4096,512]{1,0:T(8,128)(2,1)S(1)}, bf16[4096,512]{1,0:T(8,128)(2,1)}, u32[]{:S(2)}) copy-start(bf16[4096,512]{1,0:T(8,128)(2,1)} %param.9) | copy-start | bytes 12582916
  65.5 6.2 %copy-start.4 = (bf16[512,4096]{1,0:T(8,128)(2,1)S(1)}, bf16[512,4096]{1,0:T(8,128)(2,1)}, u32[]{:S(2)}) copy-start(bf16[512,4096]{1,0:T(8,128)(2,1)} %all-gather.3.cloned.1.call-done) | copy-start | bytes 12582916
  71.7 2.6 %copy-start.1 = (bf16[4096,512]{1,0:T(8,128)(2,1)S(1)}, bf16[4096,512]{1,0:T(8,128)(2,1)}, u32[]{:S(2)}) copy-start(bf16[4096,512]{1,0:T(8,128)(2,1)} %param.8) | copy-start | bytes 12582916
  81.3 27.1 %collective-permute-start.1 = (bf16[512,1024]{0,1:T(8,128)(2,1)S(1)}, bf16[512,1024]{0,1:T(8,128)(2,1)S(1)}, u32[]{:S(2)}, u32[]{:S(2)}) collective-permute-start(bf16[512,1024]{0,1:T(8,128)(2,1)S(1)} %pad_maximum_fusion), channel_id=1, source_target_pairs={{0,128},{128,0},{1,129},{129,1},{2,130},{130,2},{3,131},{131,3},{4... | collective-permute-start | bytes 3145736 | tf_op jit(solution)/shard_map/ppermute | solution.py:30
  171.9 12.0 %all-to-all-start.1 = ((bf16[8,4,4096]{2,1,0:T(4,128)(2,1)}), bf16[8,4,4096]{2,1,0:T(4,128)(2,1)S(1)}, u32[]{:S(2)}, u32[]{:S(2)}) async-start(bf16[8,4,4096]{2,1,0:T(4,128)(2,1)} %reshape.45), calls=%async_computation.2 | async-start | bytes 524288 | tf_op jit(solution)/shard_map/all_to_all | solution.py:75
Sparse Core Ops, SparseCore 0:
  22.7 42.8 all-gather.2
  67.9 37.9 all-gather.4
  108.5 61.5 reduce-scatter.1
where the time goes:
time: 192 us; the launch traced here: 191 us
  waiting for transfers between devices  116 us (60%)
  matrix products  29.9 us (16%)
  between operations  13.9 us (7%)
  local copies, waits for them, and re-layouts  12 us (6%)
  blocking collectives  12 us (6%)
  starting transfers between devices  6.69 us (3%)
    reduce_scatter x1, waiting for transfers between devices, per_device(): lax.psum_scatter(partial_value, 's', scatter_dimension=0, tiled=True)  54.6 us
    all_gather x1, waiting for transfers between devices, per_device(): rows = lax.all_gather(mine, 's', axis=0, tiled=True)  32.5 us
    all_gather x1, waiting for transfers between devices, per_device(): far_rows = lax.all_gather(far_mine, 's', axis=0, tiled=True)  17.9 us
    dot_general x2, matrix products, contract_rows(): lax.dot_general(left_rows, right_rows, (((0,), (0,)), ((), ())), preferre...  13.2 us
    all_to_all x1, blocking collectives, per_device(): lax.all_to_all(outgoing.reshape(EXPERTS, CAP, model_width), 'e', split_ax...  12 us
    ppermute x2, waiting for transfers between devices, swap_dp(): return lax.ppermute(block, 'dp', [(0, 1), (1, 0)])  8.23 us
    dot_general x1, matrix products, per_device(): gate_pre = jnp.dot(rows, gate_weight, preferred_element_type=jnp.float32)  6.13 us
    all_to_all x1, starting transfers between devices, per_device(): lax.all_to_all(summed.reshape(EXPERTS, CAP, model_width), 'e', split_axis...  5.07 us
  transfers between devices with their start and end apart: 6, of which 6 were waited for; matrix products, arithmetic and copies ran while one was open for 19% of the time, Pallas kernels for 0%

commit v1 on v0

--- a/solution.py
+++ b/solution.py
@@ -6,6 +6,15 @@
 EXPERTS = 8
 TOP = 2
 CAP = 4
+
+
+def show_slots(sheet):
+    return jnp.concatenate(
+        lax.all_to_all(
+            jnp.stack([sheet] * lax.axis_size("s")), axis_name="s", split_axis=0, concat_axis=0
+        ),
+        axis=0,
+    )
 
 
 def slot_tables(routing_dev):
@@ -48,7 +57,7 @@
         outgoing.reshape(EXPERTS, CAP, model_width), "e", split_axis=0, concat_axis=0, tiled=True
     ).reshape(EXPERTS * CAP, model_width)
     far_mine = swap_dp(lax.dynamic_slice_in_dim(mine, (1 - replica) * half, half, 1))
-    rows = lax.all_gather(mine, "s", axis=0, tiled=True)
+    rows = show_slots(mine)
     far_rows = lax.all_gather(far_mine, "s", axis=0, tiled=True)
     grad_h = (
         hidden_grad.reshape(EXPERTS, shards, CAP, ffd)

time: 192 us -> 238 us (1.24)
  waiting for transfers between devices: 116 us -> 150 us
  starting transfers between devices: 6.69 us -> 15.6 us
  matrix products: 29.9 us -> 32.3 us
    all_to_all x0 -> x1, waiting for transfers between devices: none -> 94.8 us  [show_slots(): lax.all_to_all(jnp.stack([sheet] * lax.axis_size('s')), axis_name='s', sp...]
    all_gather x1 -> x0, waiting for transfers between devices: 32.5 us -> none  [per_device(): rows = lax.all_gather(mine, 's', axis=0, tiled=True)]
    reduce_scatter x1, waiting for transfers between devices: 54.6 us -> 26.7 us  [per_device(): lax.psum_scatter(partial_value, 's', scatter_dimension=0, tiled=True)]
    ppermute x2, waiting for transfers between devices: 8.23 us -> 26.2 us  [swap_dp(): return lax.ppermute(block, 'dp', [(0, 1), (1, 0)])]
    all_gather x1, waiting for transfers between devices: 17.9 us -> 0.01 us  [per_device(): far_rows = lax.all_gather(far_mine, 's', axis=0, tiled=True)]
    all_to_all x0 -> x1, starting transfers between devices: none -> 8.75 us  [show_slots(): lax.all_to_all(jnp.stack([sheet] * lax.axis_size('s')), axis_name='s', sp...]
    another operation x0 -> x2, local copies, waits for them, and re-layouts: none -> 2.51 us  [show_slots(): jnp.stack([sheet] * lax.axis_size('s'))]
  transfers between devices with their start and end apart: 6 -> 6, of which waited for: 6 -> 5; matrix products, arithmetic and copies ran while one was open for 19% -> 16% of each run, Pallas kernels for 0% -> 0%
where the time goes in v1:
time: 238 us; the launch traced here: 237 us
  waiting for transfers between devices  150 us (63%)
  matrix products  32.3 us (14%)
  starting transfers between devices  15.6 us (7%)
  between operations  14.2 us (6%)
  blocking collectives  12 us (5%)
  local copies, waits for them, and re-layouts  11.8 us (5%)
    all_to_all x1, waiting for transfers between devices, show_slots(): lax.all_to_all(jnp.stack([sheet] * lax.axis_size('s')), axis_name='s', sp...  94.8 us
    reduce_scatter x1, waiting for transfers between devices, per_device(): lax.psum_scatter(partial_value, 's', scatter_dimension=0, tiled=True)  26.7 us
    ppermute x2, waiting for transfers between devices, swap_dp(): return lax.ppermute(block, 'dp', [(0, 1), (1, 0)])  26.2 us
    dot_general x2, matrix products, contract_rows(): lax.dot_general(left_rows, right_rows, (((0,), (0,)), ((), ())), preferre...  13.3 us
    all_to_all x1, blocking collectives, per_device(): lax.all_to_all(outgoing.reshape(EXPERTS, CAP, model_width), 'e', split_ax...  12 us
    all_to_all x1, starting transfers between devices, show_slots(): lax.all_to_all(jnp.stack([sheet] * lax.axis_size('s')), axis_name='s', sp...  8.75 us
    dot_general x1, matrix products, per_device(): gate_pre = jnp.dot(rows, gate_weight, preferred_element_type=jnp.float32)  6.12 us
    all_to_all x1, starting transfers between devices, per_device(): lax.all_to_all(summed.reshape(EXPERTS, CAP, model_width), 'e', split_axis...  5.21 us
  transfers between devices with their start and end apart: 6, of which 5 were waited for; matrix products, arithmetic and copies ran while one was open for 16% of the time, Pallas kernels for 0%

profile of v1, /device:TPU:16, one launch (start us, length us, event | category | flops | bytes accessed | tf_op | source)
XLA Modules:
  0.0 237.3 jit_solution(11352975598300916793)
XLA Ops:
  7.2 0.0 copy-start
  7.2 0.8 copy.25
  8.0 0.1 eq.29
  8.1 0.1 fusion.4
  8.1 0.1 reduce_window_sum.11
  8.2 0.2 select_reduce_fusion
  8.4 0.1 reduce_sum.21
  8.5 0.1 copy.26
  8.5 0.7 multiply_add_fusion
  9.2 0.1 convert_reduce_fusion
  9.3 0.0 copy-done
  9.3 0.2 convolution_convert_fusion
  9.6 0.1 reshape.46
  9.7 12.0 %all_to_all.15 = bf16[8,4,4096]{2,1,0:T(4,128)(2,1)S(1)} all-to-all(bf16[8,4,4096]{2,1,0:T(4,128)(2,1)S(1)} %reshape.46), channel_id=1, replica_groups=mesh['dp'=2,'e'=8,'s'=16] {'e'}, dimensions={0} | all-to-all | bytes 524288 | tf_op jit(solution)/shard_map/all_to_all | solution.py:56
  21.7 0.1 stack_reshape.2
  21.8 2.5 %stack.3 = bf16[16,32,4096]{2,1,0:T(8,128)(2,1)} broadcast(bf16[32,4096]{1,0:T(8,128)(2,1)S(1)} %stack_reshape.2), dimensions={1,2} | broadcast | bytes 4456448 | tf_op jit(solution)/shard_map/stack | solution.py:14
  24.2 8.8 %all-to-all-start.1 = ((bf16[16,32,4096]{2,1,0:T(8,128)(2,1)}), bf16[16,32,4096]{2,1,0:T(8,128)(2,1)}, u32[]{:S(2)}, u32[]{:S(2)}) async-start(bf16[16,32,4096]{2,1,0:T(8,128)(2,1)} %stack.3), calls=%async_computation.1 | async-start | bytes 8388608 | tf_op jit(solution)/shard_map/all_to_all | solution.py:13
  33.0 0.0 all-gather.2.cloned.1.call-start
  33.1 0.7 collective-permute-start
  33.8 6.6 %collective-permute-done = bf16[32,2048]{1,0:T(8,128)(2,1)S(1)} collective-permute-done((bf16[32,2048]{1,0:T(8,128)(2,1)S(1)}, bf16[32,2048]{1,0:T(8,128)(2,1)S(1)}, u32[]{:S(2)}, u32[]{:S(2)}) %collective-permute-start) | collective-permute-done | bytes 131104 | tf_op jit(solution)/shard_map/ppermute | solution.py:39
  40.4 0.7 copy-done.4
  41.1 0.0 all-gather.2.cloned.1.call-update
  41.1 0.0 reduce-scatter.2.cloned.1.call-start
  41.2 0.0 copy-done.3
  41.2 0.3 reshape.51
  41.5 0.1 copy.31
  41.6 0.4 reshape.50
  42.0 0.3 copy.28
  42.3 94.8 %all-to-all-done.1 = bf16[16,32,4096]{2,1,0:T(8,128)(2,1)} async-done(((bf16[16,32,4096]{2,1,0:T(8,128)(2,1)}), bf16[16,32,4096]{2,1,0:T(8,128)(2,1)}, u32[]{:S(2)}, u32[]{:S(2)}) %all-to-all-start.1) | async-done | bytes 4194336 | tf_op jit(solution)/shard_map/all_to_all | solution.py:13
  137.2 6.1 %multiply_convert_fusion = (bf16[512,512]{0,1:T(8,128)(2,1)S(1)}, f32[512,512]{0,1:T(8,128)S(1)}) fusion(f32[512,512]{0,1:T(8,128)S(1)} %copy.28, bf16[512,4096]{1,0:T(8,128)(2,1)} %bitcast.1, bf16[4096,512]{1,0:T(8,128)(2,1)} %param.8), kind=kOutput, calls=%fused_computation.12 | convolution fusion | flops 2149056512 | bytes 11010048 | tf_op jit(solution)/shard_map/dot_general | solution.py:68
  143.3 0.0 copy-start.1
  143.3 5.0 %fusion.3 = bf16[512,512]{0,1:T(8,128)(2,1)S(1)} fusion(f32[512,512]{0,1:T(8,128)S(1)} %copy.28, bf16[512,4096]{1,0:T(8,128)(2,1)} %bitcast.1, bf16[4096,512]{1,0:T(8,128)(2,1)S(1)} %copy-done.2, f32[512,512]{0,1:T(8,128)S(1)} %get-tuple-element.6), kind=kOutput, calls=%fused_computation.9 | convolution fusion | flops 2150105088 | bytes 11010048 | tf_op jit(solution)/shard_map/dot_general | solution.py:69
  148.3 0.0 copy-done.1
  148.3 2.4 %fusion.9 = f32[512,4096]{1,0:T(8,128)S(1)} fusion(bf16[512,512]{0,1:T(8,128)(2,1)S(1)} %fusion.3, bf16[4096,512]{1,0:T(8,128)(2,1)S(1)} %copy-done.1), kind=kOutput, calls=%fused_computation.25 | convolution fusion | flops 2147483648 | bytes 13107200 | tf_op jit(solution)/shard_map/dot_general | solution.py:76
  150.7 4.5 %add_convert_fusion.1 = bf16[512,4096]{1,0:T(8,128)(2,1)} fusion(f32[512,4096]{1,0:T(8,128)S(1)} %fusion.9, bf16[512,512]{0,1:T(8,128)(2,1)S(1)} %get-tuple-element.5, bf16[4096,512]{1,0:T(8,128)(2,1)S(1)} %copy-done.2), kind=kOutput, calls=%fused_computation.1 | convolution fusion | flops 2151677952 | bytes 17301504 | tf_op jit(solution)/shard_map/dot_general | solution.py:79
  155.2 0.0 reduce-scatter.2.cloned.1.call-update
  155.2 0.1 pad_maximum_fusion
  155.3 0.9 collective-permute-start.1
  156.2 6.0 %convolution_convert_fusion.2 = bf16[2048,1024]{1,0:T(8,128)(2,1)} fusion(bf16[512,4096]{1,0:T(8,128)(2,1)} %bitcast.1, s32[]{:T(128)S(6)} %select_n.6, bf16[512,512]{0,1:T(8,128)(2,1)S(1)} %get-tuple-element.5, bf16[512,512]{0,1:T(8,128)(2,1)S(1)} %fusion.3), kind=kOutput, calls=%fused_computation.4 | convolution fusion | flops 2151677952 | bytes 7340036 | tf_op jit(solution)/shard_map/dot_general | solution.py:33
  162.1 19.5 %collective-permute-done.1 = bf16[512,1024]{0,1:T(8,128)(2,1)S(1)} collective-permute-done((bf16[512,1024]{0,1:T(8,128)(2,1)S(1)}, bf16[512,1024]{0,1:T(8,128)(2,1)S(1)}, u32[]{:S(2)}, u32[]{:S(2)}) %collective-permute-start.1) | collective-permute-done | bytes 1048608 | tf_op jit(solution)/shard_map/ppermute | solution.py:39
  181.6 7.3 %add_convert_fusion = bf16[2048,1024]{1,0:T(8,128)(2,1)} fusion(bf16[2048,1024]{1,0:T(8,128)(2,1)} %convolution_convert_fusion.2, bf16[512,2048]{1,0:T(8,128)(2,1)} %all-gather.2.cloned.1.call-done, bf16[512,1024]{0,1:T(8,128)(2,1)S(1)} %collective-permute-done.1), kind=kOutput, calls=%fused_computation | convolution fusion | flops 2153775104 | bytes 11534336 | tf_op jit(solution)/shard_map/dot_general | solution.py:33
  188.9 26.7 %reduce-scatter.2.cloned.1.call-done = bf16[32,4096]{1,0:T(8,128)(2,1)} async-done(((bf16[512,4096]{1,0:T(8,128)(2,1)}), bf16[32,4096]{1,0:T(8,128)(2,1)}) %reduce-scatter.2.cloned.1.call-update) | async-done | bytes 262160 | tf_op jit(solution)/shard_map/reduce_scatter | solution.py:83
  215.7 1.8 reshape.48
  217.4 5.2 %all-to-all-start.2 = ((bf16[8,4,4096]{2,1,0:T(4,128)(2,1)}), bf16[8,4,4096]{2,1,0:T(4,128)(2,1)S(1)}, u32[]{:S(2)}, u32[]{:S(2)}) async-start(bf16[8,4,4096]{2,1,0:T(4,128)(2,1)} %reshape.48), calls=%async_computation.3 | async-start | bytes 524288 | tf_op jit(solution)/shard_map/all_to_all | solution.py:84
  222.6 4.5 %fusion.8 = (bf16[2048,512]{1,0:T(8,128)(2,1)}, bf16[2048,512]{1,0:T(8,128)(2,1)}) fusion(bf16[2048,1024]{1,0:T(8,128)(2,1)} %add_convert_fusion), kind=kLoop, calls=%fused_computation.24 | loop fusion | bytes 8388608 | tf_op jit(solution)/shard_map/slice | solution.py:96
  227.1 2.4 %all-to-all-done.2 = bf16[8,4,4096]{2,1,0:T(4,128)(2,1)S(1)} async-done(((bf16[8,4,4096]{2,1,0:T(4,128)(2,1)}), bf16[8,4,4096]{2,1,0:T(4,128)(2,1)S(1)}, u32[]{:S(2)}, u32[]{:S(2)}) %all-to-all-start.2) | async-done | bytes 262176 | tf_op jit(solution)/shard_map/all_to_all | solution.py:84
  229.6 0.1 reshape.49
  229.6 0.8 convolution_convert_fusion.1
  (6 shorter events, 0.0 us)
Async XLA Ops:
  7.2 2.2 copy-start
  24.2 16.9 %copy-start.3 = (bf16[512,512]{1,0:T(8,128)(2,1)S(1)}, bf16[512,512]{1,0:T(8,128)(2,1)}, u32[]{:S(2)}) copy-start(bf16[512,512]{1,0:T(8,128)(2,1)} %param.7) | copy-start | bytes 1572868
  24.2 112.9 %all-to-all-start.1 = ((bf16[16,32,4096]{2,1,0:T(8,128)(2,1)}), bf16[16,32,4096]{2,1,0:T(8,128)(2,1)}, u32[]{:S(2)}, u32[]{:S(2)}) async-start(bf16[16,32,4096]{2,1,0:T(8,128)(2,1)} %stack.3), calls=%async_computation.1 | async-start | bytes 8388608 | tf_op jit(solution)/shard_map/all_to_all | solution.py:13
  33.0 129.1 %all-gather.2.cloned.1.call-start = ((), (), s32[]{:S(2)}) async-start(), calls=%async_computation.5 | async-start | bytes 2228224 | tf_op jit(solution)/shard_map/all_gather | solution.py:61
  33.1 7.3 %collective-permute-start = (bf16[32,2048]{1,0:T(8,128)(2,1)S(1)}, bf16[32,2048]{1,0:T(8,128)(2,1)S(1)}, u32[]{:S(2)}, u32[]{:S(2)}) collective-permute-start(bf16[32,2048]{1,0:T(8,128)(2,1)S(1)} %constant_dynamic-slice_fusion), channel_id=1, source_target_pairs={{0,128},{128,0},{1,129},{129,1},{2,130},{130,2},{3,131},{131,3},{4... | collective-permute-start | bytes 393224 | tf_op jit(solution)/shard_map/ppermute | solution.py:39
  40.4 0.7 copy-start.4
  41.1 174.5 %reduce-scatter.2.cloned.1.call-start = ((), (), s32[]{:S(2)}) async-start(), calls=%async_computation.4 | async-start | bytes 4456448 | tf_op jit(solution)/shard_map/reduce_scatter | solution.py:83
  137.2 6.1 %copy-start.2 = (bf16[4096,512]{1,0:T(8,128)(2,1)S(1)}, bf16[4096,512]{1,0:T(8,128)(2,1)}, u32[]{:S(2)}) copy-start(bf16[4096,512]{1,0:T(8,128)(2,1)} %param.9) | copy-start | bytes 12582916
  143.3 5.0 %copy-start.1 = (bf16[4096,512]{1,0:T(8,128)(2,1)S(1)}, bf16[4096,512]{1,0:T(8,128)(2,1)}, u32[]{:S(2)}) copy-start(bf16[4096,512]{1,0:T(8,128)(2,1)} %param.8) | copy-start | bytes 12582916
  155.3 26.4 %collective-permute-start.1 = (bf16[512,1024]{0,1:T(8,128)(2,1)S(1)}, bf16[512,1024]{0,1:T(8,128)(2,1)S(1)}, u32[]{:S(2)}, u32[]{:S(2)}) collective-permute-start(bf16[512,1024]{0,1:T(8,128)(2,1)S(1)} %pad_maximum_fusion), channel_id=1, source_target_pairs={{0,128},{128,0},{1,129},{129,1},{2,130},{130,2},{3,131},{131,3},{4... | collective-permute-start | bytes 3145736 | tf_op jit(solution)/shard_map/ppermute | solution.py:39
  217.4 12.1 %all-to-all-start.2 = ((bf16[8,4,4096]{2,1,0:T(4,128)(2,1)}), bf16[8,4,4096]{2,1,0:T(4,128)(2,1)S(1)}, u32[]{:S(2)}, u32[]{:S(2)}) async-start(bf16[8,4,4096]{2,1,0:T(4,128)(2,1)} %reshape.48), calls=%async_computation.3 | async-start | bytes 524288 | tf_op jit(solution)/shard_map/all_to_all | solution.py:84
Sparse Core Ops, SparseCore 0:
  41.2 63.0 all-gather.1
  155.3 60.3 reduce-scatter.1
